TPU v7x, 256 devices: a whole 4x4x8 slice. The times are simulated.
256 devices in a mesh: head: 8 (over x_hi, y), tok: 32 (over z, x_lo, core).
Axes of the slice: x: 4 (x_hi: 2, x_lo: 2; x = x_hi * 2 + x_lo), y: 4, z: 8, core: 2. Of those that a mesh axis runs over, the one named last changes fastest.
Arguments:
- tokens: bfloat16 [16384, 8192], P('tok', 'head'), may hold values from -20 to 20
- qkv_maps: bfloat16 [16, 512, 1536], P('head'), may hold values from -0.26516504 to 0.26516504
- rate_map: bfloat16 [8192, 16], P('head'), may hold values from -0.09375 to 0.09375
- fast_init: bfloat16 [16, 3, 512, 512], P('head'), may hold values from -0.25 to 0.25
Outputs:
- layer_out: bfloat16 [16384, 8192], P('tok', 'head')
All inputs are finite; a program needn't handle non-finite values.
Results may differ from a plain program's by a relative error of at most 0.04.
Values may be sent and summed in bfloat16 or wider, within the bound.
A program may use at most 128 MiB of HBM per device.

v0:
```python
import jax
import jax.numpy as jnp
from jax import lax
from jax.sharding import PartitionSpec as P

WINDOW = 512


rate_base = 0.003
epsilon = 1e-06


def from_behind(block, axis, distance):
    devices = range(lax.axis_size(axis))
    route = [(i - distance, i) for i in devices if i - distance in devices]
    return lax.ppermute(block, axis, route)


def rms_rows(matrix):
    matrix = matrix.astype(jnp.float32)
    return matrix / jnp.sqrt(jnp.mean(matrix * matrix, axis=-1, keepdims=True) + epsilon)


def renorm(updated, initial):
    target = jnp.sqrt(jnp.mean(initial * initial, axis=-1, keepdims=True) + epsilon)
    current = jnp.sqrt(jnp.mean(updated * updated, axis=-1, keepdims=True) + epsilon)
    return (updated * (target / current)).astype(jnp.bfloat16)


def band_attention(queries, key_rows, value_rows, query_pos, key_pos, score_scale):
    scores = (
        jnp.einsum("qhd,khd->hqk", queries, key_rows, preferred_element_type=jnp.float32)
        * score_scale
    )
    key_mask = (
        (key_pos[None, :] <= query_pos[:, None])
        & (key_pos[None, :] > query_pos[:, None] - WINDOW)
        & (key_pos[None, :] >= 0)
    )
    key_mask = key_mask[None]
    row_max = jnp.max(jnp.where(key_mask, scores, -1e30), axis=2, keepdims=True)
    raised = jnp.where(key_mask, jnp.exp(scores - row_max), 0.0)
    probs = (raised / jnp.sum(raised, axis=2, keepdims=True)).astype(jnp.bfloat16)
    return jnp.einsum("hqk,khd->qhd", probs, value_rows, preferred_element_type=jnp.float32)


def fast_gradient(weights, key_part, value_part, rate_part):
    pre_gate = jnp.einsum(
        "rhd,hde->rhe", key_part, weights[:, 0], preferred_element_type=jnp.float32
    )
    pre_up = jnp.einsum("rhd,hde->rhe", key_part, weights[:, 1], preferred_element_type=jnp.float32)
    sigma = jax.nn.sigmoid(pre_gate)
    gated = pre_gate * sigma
    hidden = (gated * pre_up).astype(jnp.bfloat16)
    target = (rate_part.astype(jnp.float32)[:, :, None] * value_part.astype(jnp.float32)).astype(
        jnp.bfloat16
    )
    grad_down = jnp.einsum("rhe,rhd->hed", hidden, target, preferred_element_type=jnp.float32)
    back_hidden = jnp.einsum(
        "rhd,hed->rhe", target, weights[:, 2], preferred_element_type=jnp.float32
    )
    gate_delta = (back_hidden * pre_up * sigma * (1.0 + pre_gate * (1.0 - sigma))).astype(
        jnp.bfloat16
    )
    up_delta = (back_hidden * gated).astype(jnp.bfloat16)
    grad_gate = jnp.einsum("rhd,rhe->hde", key_part, gate_delta, preferred_element_type=jnp.float32)
    grad_up = jnp.einsum("rhd,rhe->hde", key_part, up_delta, preferred_element_type=jnp.float32)
    return jnp.stack([grad_gate, grad_up, grad_down], 1)


def fast_apply(weights, query_part):
    app_gate = jnp.einsum(
        "rhd,hde->rhe", query_part, weights[:, 0], preferred_element_type=jnp.float32
    )
    app_up = jnp.einsum(
        "rhd,hde->rhe", query_part, weights[:, 1], preferred_element_type=jnp.float32
    )
    app_hidden = (app_gate * jax.nn.sigmoid(app_gate) * app_up).astype(jnp.bfloat16)
    result = jnp.einsum(
        "rhe,hed->rhd", app_hidden, weights[:, 2], preferred_element_type=jnp.float32
    )
    return result.astype(jnp.bfloat16)


def update_weights(weights, partial_value, initial):
    total = lax.psum(partial_value.astype(jnp.bfloat16), "tok").astype(jnp.float32)
    return renorm(weights.astype(jnp.float32) + total, initial)


def body(tokens, qkv_maps, rate_map, fast_init):
    tok_rows = tokens.shape[0]
    head_count = qkv_maps.shape[0]
    head_width = qkv_maps.shape[1]
    logit_terms = jnp.dot(tokens, rate_map, preferred_element_type=jnp.float32)
    logits = lax.psum_scatter(
        logit_terms.astype(jnp.bfloat16), "head", scatter_dimension=1, tiled=True
    ).astype(jnp.float32)
    rate = (rate_base * jax.nn.softplus(logits)).astype(jnp.bfloat16)
    inputs = tokens.reshape(tok_rows, head_count, head_width)
    projected = jnp.einsum("rhd,hde->rhe", inputs, qkv_maps, preferred_element_type=jnp.float32)
    queries = projected[:, :, :head_width].astype(jnp.bfloat16)
    key_rows = projected[:, :, head_width : 2 * head_width].astype(jnp.bfloat16)
    value_rows = projected[:, :, 2 * head_width :].astype(jnp.bfloat16)
    tail_rows = min(WINDOW, tok_rows)
    edge = jnp.stack([key_rows, value_rows], 0)
    distance = 0
    received = [from_behind(edge, "tok", distance + 1)]
    anchor = lax.axis_index("tok") * tok_rows
    offsets = jnp.arange(tail_rows, dtype=jnp.int32)
    distance = 1
    arrived = received[distance - 1]
    key_parts = [arrived[0]]
    value_parts = [arrived[1]]
    position_parts = [anchor - distance * tok_rows + tok_rows - tail_rows + offsets]
    local_pos = anchor + jnp.arange(tok_rows, dtype=jnp.int32)
    all_keys = jnp.concatenate(key_parts + [key_rows], 0)
    all_values = jnp.concatenate(value_parts + [value_rows], 0)
    all_pos = jnp.concatenate(position_parts + [local_pos], 0)
    attended = band_attention(
        queries, all_keys, all_values, local_pos, all_pos, head_width ** (-0.5)
    )
    q_norm = rms_rows(queries).astype(jnp.bfloat16)
    k_norm = rms_rows(key_rows).astype(jnp.bfloat16)
    initial = fast_init.astype(jnp.float32)
    weights = fast_init
    moved_q, moved_k, moved_v, moved_rate = (
        lax.all_to_all(q_norm, "tok", split_axis=0, concat_axis=0, tiled=True),
        lax.all_to_all(k_norm, "tok", split_axis=0, concat_axis=0, tiled=True),
        lax.all_to_all(value_rows, "tok", split_axis=0, concat_axis=0, tiled=True),
        lax.all_to_all(rate, "tok", split_axis=0, concat_axis=0, tiled=True),
    )
    half_rows = tok_rows // 2
    outputs = []
    for half_index in range(2):
        first = half_index * half_rows
        partial_value = fast_gradient(
            weights,
            moved_k[first : first + half_rows],
            moved_v[first : first + half_rows],
            moved_rate[first : first + half_rows],
        )
        weights = update_weights(weights, partial_value, initial)
        outputs.append(fast_apply(weights, moved_q[first : first + half_rows]))
    fast_out = lax.all_to_all(
        jnp.concatenate(outputs, 0), "tok", split_axis=0, concat_axis=0, tiled=True
    )
    combined = (attended + fast_out.astype(jnp.float32)).astype(jnp.bfloat16)
    return combined.reshape(tok_rows, head_count * head_width)


def solution(mesh):
    in_specs = (
        P("tok", "head"),
        P("head", None, None),
        P("head", None),
        P("head", None, None, None),
    )
    out_specs = P("tok", "head")
    return jax.shard_map(body, mesh=mesh, in_specs=in_specs, out_specs=out_specs, check_vma=False)
```

profile of v0, /device:TPU:162, one launch (start us, length us, event | category | flops | bytes accessed | tf_op | source)
XLA Modules:
  0.0 706.5 jit_solution(9291676069857126913)
XLA Ops:
  8.3 41.1 %all-reduce = bf16[512,16]{0,1:T(8,128)(2,1)S(1)} all-reduce(bf16[512,16]{0,1:T(8,128)(2,1)S(1)} %convolution_convert_fusion.9), channel_id=2, replica_groups=mesh['head'=8,'tok'=32] {'head'}, use_global_device_ids=true, to_apply=%region_3.4.clone | all-reduce | flops 8192 | bytes 32768
  52.1 7.8 %all-to-all-start.1 = ((bf16[32,16,2]{1,2,0:T(2,128)(2,1)}), bf16[32,16,2]{1,2,0:T(2,128)(2,1)S(1)}, u32[]{:S(2)}, u32[]{:S(2)}) async-start(bf16[32,16,2]{1,2,0:T(2,128)(2,1)} %copy.164), calls=%async_computation.1 | async-start | bytes 32768 | tf_op jit(solution)/shard_map/all_to_all | solution.py:130
  59.9 3.6 fusion.4
  65.9 3.8 copy.162
  69.7 8.3 %all-to-all-start = ((bf16[512,2,512]{2,1,0:T(2,128)(2,1)}), bf16[512,2,512]{2,1,0:T(2,128)(2,1)}, u32[]{:S(2)}, u32[]{:S(2)}) async-start(bf16[512,2,512]{2,1,0:T(2,128)(2,1)} %copy.162), calls=%async_computation | async-start | bytes 2097152 | tf_op jit(solution)/shard_map/all_to_all | solution.py:128
  78.0 2.2 slice_bitcast_fusion.26
  80.2 3.9 copy.166
  84.1 18.9 %all-to-all-done = bf16[512,2,512]{2,1,0:T(2,128)(2,1)} async-done(((bf16[512,2,512]{2,1,0:T(2,128)(2,1)}), bf16[512,2,512]{2,1,0:T(2,128)(2,1)}, u32[]{:S(2)}, u32[]{:S(2)}) %all-to-all-start) | async-done | bytes 1048608 | tf_op jit(solution)/shard_map/all_to_all | solution.py:128
  103.0 8.2 %all-to-all-start.2 = ((bf16[512,2,512]{2,1,0:T(2,128)(2,1)}), bf16[512,2,512]{2,1,0:T(2,128)(2,1)}, u32[]{:S(2)}, u32[]{:S(2)}) async-start(bf16[512,2,512]{2,1,0:T(2,128)(2,1)} %copy.166), calls=%async_computation.2 | async-start | bytes 2097152 | tf_op jit(solution)/shard_map/all_to_all | solution.py:129
  111.4 2.7 fusion.92
  117.0 19.2 %all-to-all-done.2 = bf16[512,2,512]{2,1,0:T(2,128)(2,1)} async-done(((bf16[512,2,512]{2,1,0:T(2,128)(2,1)}), bf16[512,2,512]{2,1,0:T(2,128)(2,1)}, u32[]{:S(2)}, u32[]{:S(2)}) %all-to-all-start.2) | async-done | bytes 1048608 | tf_op jit(solution)/shard_map/all_to_all | solution.py:129
  136.2 2.9 fusion.91
  144.6 223.7 %all-reduce.4.cloned.1.call-done = bf16[2,3,512,512]{3,2,0,1:T(8,128)(2,1)} async-done(((bf16[2,3,512,512]{3,2,0,1:T(8,128)(2,1)}), bf16[2,3,512,512]{3,2,0,1:T(8,128)(2,1)}) %all-reduce.4.cloned.1.call-update) | async-done | bytes 3145744 | tf_op jit(solution)/shard_map/psum | solution.py:86
  368.4 3.6 fusion.1
  378.8 3.7 copy.174
  382.5 15.6 %all-to-all-start.3 = ((bf16[512,2,512]{2,1,0:T(2,128)(2,1)}), bf16[512,2,512]{2,1,0:T(2,128)(2,1)}, u32[]{:S(2)}, u32[]{:S(2)}) async-start(bf16[512,2,512]{2,1,0:T(2,128)(2,1)} %copy.174), calls=%async_computation.3 | async-start | bytes 2097152 | tf_op jit(solution)/shard_map/all_to_all | solution.py:127
  398.1 3.1 pad_maximum_fusion.2
  403.2 21.7 %all-to-all-done.3 = bf16[512,2,512]{2,1,0:T(2,128)(2,1)} async-done(((bf16[512,2,512]{2,1,0:T(2,128)(2,1)}), bf16[512,2,512]{2,1,0:T(2,128)(2,1)}, u32[]{:S(2)}, u32[]{:S(2)}) %all-to-all-start.3) | async-done | bytes 1048608 | tf_op jit(solution)/shard_map/all_to_all | solution.py:127
  424.9 2.7 fusion.90
  429.9 3.0 fusion.35
  432.9 204.8 %all-reduce.6.cloned.1.call-done = bf16[2,3,512,512]{3,2,0,1:T(8,128)(2,1)} async-done(((bf16[2,3,512,512]{3,2,0,1:T(8,128)(2,1)}), bf16[2,3,512,512]{3,2,0,1:T(8,128)(2,1)}) %all-reduce.6.cloned.1.call-update) | async-done | bytes 3145744 | tf_op jit(solution)/shard_map/psum | solution.py:86
  637.7 3.1 multiply_reduce_fusion
  644.0 2.5 fusion.36
  646.6 2.0 copy.196
  648.7 15.7 %all-to-all-start.4 = ((bf16[512,2,512]{2,1,0:T(2,128)(2,1)}), bf16[512,2,512]{2,1,0:T(2,128)(2,1)S(1)}, u32[]{:S(2)}, u32[]{:S(2)}) async-start(bf16[512,2,512]{2,1,0:T(2,128)(2,1)} %copy.196), calls=%async_computation.4 | async-start | bytes 2097152 | tf_op jit(solution)/shard_map/all_to_all | solution.py:144
  665.0 2.7 slice_bitcast_fusion.17
  667.6 2.5 fusion.15
  670.1 3.9 fusion.94
  674.1 15.2 %all-to-all-done.4 = bf16[512,2,512]{2,1,0:T(2,128)(2,1)S(1)} async-done(((bf16[512,2,512]{2,1,0:T(2,128)(2,1)}), bf16[512,2,512]{2,1,0:T(2,128)(2,1)S(1)}, u32[]{:S(2)}, u32[]{:S(2)}) %all-to-all-start.4) | async-done | bytes 1048608 | tf_op jit(solution)/shard_map/all_to_all | solution.py:144
  689.3 2.5 copy.197
  691.8 5.6 fusion.19
  697.4 2.3 copy.198
  (84 shorter events, 29.5 us)
Async XLA Ops:
  6.5 53.4 %copy-start = (bf16[2,512,1536]{2,1,0:T(8,128)(2,1)S(1)}, bf16[2,512,1536]{2,1,0:T(8,128)(2,1)}, u32[]{:S(2)}) copy-start(bf16[2,512,1536]{2,1,0:T(8,128)(2,1)} %param.5) | copy-start | bytes 9437188
  52.1 17.6 %all-to-all-start.1 = ((bf16[32,16,2]{1,2,0:T(2,128)(2,1)}), bf16[32,16,2]{1,2,0:T(2,128)(2,1)S(1)}, u32[]{:S(2)}, u32[]{:S(2)}) async-start(bf16[32,16,2]{1,2,0:T(2,128)(2,1)} %copy.164), calls=%async_computation.1 | async-start | bytes 32768 | tf_op jit(solution)/shard_map/all_to_all | solution.py:130
  63.5 2.4 copy-start.2
  65.9 12.2 %copy-start.3 = (bf16[512,2,1536]{0,2,1:T(8,128)(2,1)S(1)}, bf16[512,2,1536]{0,2,1:T(8,128)(2,1)}, u32[]{:S(2)}) copy-start(bf16[512,2,1536]{0,2,1:T(8,128)(2,1)} %copy-done.2) | copy-start | bytes 9437188
  69.7 33.4 %all-to-all-start = ((bf16[512,2,512]{2,1,0:T(2,128)(2,1)}), bf16[512,2,512]{2,1,0:T(2,128)(2,1)}, u32[]{:S(2)}, u32[]{:S(2)}) async-start(bf16[512,2,512]{2,1,0:T(2,128)(2,1)} %copy.162), calls=%async_computation | async-start | bytes 2097152 | tf_op jit(solution)/shard_map/all_to_all | solution.py:128
  80.2 33.9 %copy-start.4 = (bf16[2,3,512,512]{3,2,1,0:T(8,128)(2,1)S(1)}, bf16[2,3,512,512]{3,2,1,0:T(8,128)(2,1)}, u32[]{:S(2)}) copy-start(bf16[2,3,512,512]{3,2,1,0:T(8,128)(2,1)} %param.7) | copy-start | bytes 9437188
  103.0 33.2 %all-to-all-start.2 = ((bf16[512,2,512]{2,1,0:T(2,128)(2,1)}), bf16[512,2,512]{2,1,0:T(2,128)(2,1)}, u32[]{:S(2)}, u32[]{:S(2)}) async-start(bf16[512,2,512]{2,1,0:T(2,128)(2,1)} %copy.166), calls=%async_computation.2 | async-start | bytes 2097152 | tf_op jit(solution)/shard_map/all_to_all | solution.py:129
  111.3 257.1 %all-reduce.4.cloned.1.call-start = ((), (), s32[]{:S(2)}) async-start(), calls=%async_computation.5 | async-start | bytes 6291456 | tf_op jit(solution)/shard_map/psum | solution.py:86
  114.2 1.4 copy-start.15
  136.2 3.3 copy-start.16
  136.2 3.3 copy-start.17
  139.6 1.2 copy-start.18
  144.3 493.4 %all-reduce.6.cloned.1.call-start = ((), (), s32[]{:S(2)}) async-start(), calls=%async_computation.6 | async-start | bytes 6291456 | tf_op jit(solution)/shard_map/psum | solution.py:86
  368.4 3.6 copy-start.5
  368.4 3.8 copy-start.6
  372.1 1.0 copy-start.9
  373.1 1.1 copy-start.13
  382.5 42.4 %all-to-all-start.3 = ((bf16[512,2,512]{2,1,0:T(2,128)(2,1)}), bf16[512,2,512]{2,1,0:T(2,128)(2,1)}, u32[]{:S(2)}, u32[]{:S(2)}) async-start(bf16[512,2,512]{2,1,0:T(2,128)(2,1)} %copy.174), calls=%async_computation.3 | async-start | bytes 2097152 | tf_op jit(solution)/shard_map/all_to_all | solution.py:127
  401.2 263.8 %collective-permute-start = (bf16[2,512,2,512]{1,3,2,0:T(8,128)(2,1)}, bf16[2,512,2,512]{1,3,2,0:T(8,128)(2,1)}, u32[]{:S(2)}, u32[]{:S(2)}) collective-permute-start(bf16[2,512,2,512]{1,3,2,0:T(8,128)(2,1)} %pad_maximum_fusion.2), channel_id=1, source_target_pairs={{0,1},{1,2},{2,3},{3,4},{4,5},{5,6},{6,7},{7,8},{8,9},{9,10},{10,1... | collective-permute-start | bytes 6291464 | tf_op jit(solution)/shard_map/ppermute | solution.py:16
  427.7 0.8 copy-start.12
  637.7 3.2 copy-start.7
  640.9 2.7 copy-start.11
  641.9 1.7 copy-start.8
  644.0 2.5 copy-start.14
  648.7 19.0 %copy-start.10 = (bf16[512,2,512]{0,2,1:T(8,128)(2,1)S(1)}, bf16[512,2,512]{0,2,1:T(8,128)(2,1)}, u32[]{:S(2)}) copy-start(bf16[512,2,512]{0,2,1:T(8,128)(2,1)} %get-tuple-element.12) | copy-start | bytes 3145732
  648.7 40.6 %all-to-all-start.4 = ((bf16[512,2,512]{2,1,0:T(2,128)(2,1)}), bf16[512,2,512]{2,1,0:T(2,128)(2,1)S(1)}, u32[]{:S(2)}, u32[]{:S(2)}) async-start(bf16[512,2,512]{2,1,0:T(2,128)(2,1)} %copy.196), calls=%async_computation.4 | async-start | bytes 2097152 | tf_op jit(solution)/shard_map/all_to_all | solution.py:144
  691.8 7.9 %copy-start.1 = (bf16[2,512,1536]{2,1,0:T(8,128)(2,1)S(1)}, bf16[2,512,1536]{2,1,0:T(8,128)(2,1)}, u32[]{:S(2)}) copy-start(bf16[2,512,1536]{2,1,0:T(8,128)(2,1)} %param.5) | copy-start | bytes 9437188
Sparse Core Ops, SparseCore 0:
  144.4 223.8 all-reduce.3
  379.0 258.6 all-reduce.5
where the time goes:
time: 714 us; the launch traced here: 707 us
  waiting for transfers between devices  504 us (71%)
  starting transfers between devices  57.9 us (8%)
  blocking collectives  41.1 us (6%)
  local copies, waits for them, and re-layouts  36.9 us (5%)
  matrix products  29.6 us (4%)
  other arithmetic  22.9 us (3%)
  between operations  14.5 us (2%)
    psum x2, waiting for transfers between devices, update_weights(): lax.psum(partial_value.astype(jnp.bfloat16), 'tok').astype(jnp.float32)  429 us
    unnamed x1, blocking collectives  41.1 us
    all_to_all x1, waiting for transfers between devices, body(): lax.all_to_all(q_norm, 'tok', split_axis=0, concat_axis=0, tiled=True)  21.7 us
    all_to_all x1, waiting for transfers between devices, body(): lax.all_to_all(value_rows, 'tok', split_axis=0, concat_axis=0, tiled=True)  19.2 us
    all_to_all x1, waiting for transfers between devices, body(): lax.all_to_all(k_norm, 'tok', split_axis=0, concat_axis=0, tiled=True)  18.9 us
    all_to_all x1, starting transfers between devices, body(): lax.all_to_all(jnp.concatenate(outputs, 0), 'tok', split_axis=0, concat_a...  15.7 us
    all_to_all x1, starting transfers between devices, body(): lax.all_to_all(q_norm, 'tok', split_axis=0, concat_axis=0, tiled=True)  15.6 us
    all_to_all x1, waiting for transfers between devices, body(): lax.all_to_all(jnp.concatenate(outputs, 0), 'tok', split_axis=0, concat_a...  15.2 us
  transfers between devices with their start and end apart: 8, of which 6 were waited for; matrix products, arithmetic and copies ran while one was open for 8% of the time, Pallas kernels for 0%

commit v1 on v0

v1 whole, which is shorter than its diff:
```python
import functools

import jax
import jax.numpy as jnp
from jax import lax
from jax.experimental import pallas as pl
from jax.experimental.pallas import tpu as pltpu
from jax.sharding import PartitionSpec as P

MESH = pl.DeviceIdType.MESH
WINDOW = 512
HD = 512
HALF = 256
ROWS = 512
NC = 8
NZ = 8
NH = 8
CH = 96

rate_base = 0.003
epsilon = 1e-06

bf16 = jnp.bfloat16
f32 = jnp.float32


def dot(a, b):
    return jnp.dot(a, b, preferred_element_type=f32)


def dot_t(a, b):
    return lax.dot_general(a, b, (((1,), (1,)), ((), ())), preferred_element_type=f32)


def dot_l(a, b):
    return lax.dot_general(a, b, (((0,), (0,)), ((), ())), preferred_element_type=f32)


def softplus(a):
    return jnp.maximum(a, 0.0) + jnp.log1p(jnp.exp(-jnp.abs(a)))


def rms(m):
    m = m.astype(f32)
    return (m * lax.rsqrt(jnp.mean(m * m, axis=-1, keepdims=True) + epsilon)).astype(bf16)


def learn_kernel(
    tok_ref, maps_ref, rmap_ref, init_ref,
    wall, halo,
    xbuf, knb, vb, dbuf, g13, g2, rbuf, sbuf, wp, wcur, ss_s, ss_r,
    rcol, lgs, lgr, rates,
    xp_s, xp_r, xx_s, xx_r, xf_s, xf_r, lg_s, lg_r, rt_s, rt_r,
    rs_s, rs_r, sp_s, sp_r, wn_s, wn_r, wc_s, wc_r,
    dp_s, dp_r, dx_s, dx_r, df_s, df_r, ha_s, ha_r,
):
    head = lax.axis_index("head")
    tok = lax.axis_index("tok")
    z = tok // 4
    x = (tok // 2) % 2
    c = tok % 2
    p = z % 4
    s = z // 4
    b_me = x * 2 + c

    def at(zz, xx, cc):
        return (head, zz * 4 + xx * 2 + cc)

    up = at((z + 1) % NZ, x, c)
    down = at((z + NZ - 1) % NZ, x, c)
    mate = at(z, x, 1 - c)
    side = at(z, 1 - x, c)
    diag = at(z, 1 - x, 1 - c)
    tok_next = (head, (tok + 1) % 32)
    tok_prev = (head, (tok + 31) % 32)

    barrier = pltpu.get_barrier_semaphore()
    peers = [up, down, mate, side, diag, tok_next, tok_prev]
    peers += [((head + o) % NH, tok) for o in range(1, NH)]
    for peer in peers:
        pl.semaphore_signal(barrier, inc=1, device_id=peer, device_id_type=MESH)
    pl.semaphore_wait(barrier, len(peers))

    def rcopy(src, dst, ssem, rsem, dev):
        return pltpu.make_async_remote_copy(
            src_ref=src, dst_ref=dst, send_sem=ssem, recv_sem=rsem,
            device_id=dev, device_id_type=MESH,
        )

    mine = pl.ds(pl.multiple_of(x * HD, HD), HD)
    other = pl.ds(pl.multiple_of((1 - x) * HD, HD), HD)

    def x_send(j):
        return rcopy(
            tok_ref.at[pl.ds(j * 128, 128), other],
            xbuf.at[b_me, pl.ds(j * 128, 128)],
            xx_s.at[j], xx_r.at[j], side,
        )

    def x_recv(j):
        return rcopy(
            tok_ref.at[pl.ds(j * 128, 128), other],
            xbuf.at[(1 - x) * 2 + c, pl.ds(j * 128, 128)],
            xx_s.at[j], xx_r.at[j], side,
        )

    def f_send(j):
        blk = xbuf.at[(1 - x) * 2 + c, pl.ds(j * 128, 128)]
        return rcopy(blk, blk, xf_s.at[j], xf_r.at[j], mate)

    def f_recv(j):
        blk = xbuf.at[(1 - x) * 2 + 1 - c, pl.ds(j * 128, 128)]
        return rcopy(blk, blk, xf_s.at[j], xf_r.at[j], mate)

    p_send = rcopy(tok_ref.at[:, mine], xbuf.at[b_me], xp_s, xp_r, mate)
    p_recv = rcopy(tok_ref.at[:, mine], xbuf.at[x * 2 + 1 - c], xp_s, xp_r, mate)
    for j in range(4):
        x_send(j).start()
    p_send.start()
    xbuf[b_me] = tok_ref[:, mine]

    part = lax.dot_general(
        rmap_ref[...], tok_ref[...], (((0,), (1,)), ((), ())), preferred_element_type=f32
    )
    for q in range(NH):
        lgs[q] = jnp.concatenate([part[2 * q : 2 * q + 2], jnp.zeros((6, ROWS), f32)], 0)

    def lg_copy(o):
        peer = (head + o) % NH
        return rcopy(lgs.at[peer], lgr.at[head], lg_s.at[o - 1], lg_r.at[head], (peer, tok))

    def lg_wait(o):
        src = (head + o) % NH
        return rcopy(lgs.at[src], lgr.at[src], lg_s.at[o - 1], lg_r.at[src], (src, tok))

    for o in range(1, NH):
        lg_copy(o).start()
    lgr[head] = lgs[head]

    def keys_values(b):
        def step(i, carry):
            rows = pl.ds(pl.multiple_of(i * 256, 256), 256)
            xb = xbuf[b, rows]
            out = pl.ds(pl.multiple_of(b * ROWS + i * 256, 256), 256)
            knb[out] = rms(dot(xb, maps_ref[x, :, HD : 2 * HD]).astype(bf16))
            vb[out] = dot(xb, maps_ref[x, :, 2 * HD :]).astype(bf16)
            return carry

        lax.fori_loop(0, 2, step, 0)

    keys_values(b_me)

    for o in range(1, NH):
        lg_wait(o).wait_recv()
    total = lgr[0]
    for q in range(1, NH):
        total = total + lgr[q]
    rates[b_me] = (rate_base * softplus(total)).astype(bf16).astype(f32)
    group = [(mate, x * 2 + 1 - c), (side, (1 - x) * 2 + c), (diag, (1 - x) * 2 + 1 - c)]

    def rt_copy(i):
        dev, _ = group[i]
        return rcopy(rates.at[b_me], rates.at[b_me], rt_s.at[i], rt_r.at[b_me], dev)

    def rt_wait(i):
        dev, src = group[i]
        return rcopy(rates.at[src], rates.at[src], rt_s.at[i], rt_r.at[src], dev)

    for i in range(3):
        rt_copy(i).start()

    p_recv.wait_recv()
    keys_values(x * 2 + 1 - c)
    for j in range(4):
        x_recv(j).wait_recv()
        f_send(j).start()
    keys_values((1 - x) * 2 + c)
    for j in range(4):
        f_recv(j).wait_recv()
    keys_values((1 - x) * 2 + 1 - c)

    for i in range(3):
        rt_wait(i).wait_recv()
    for b in range(4):
        row = jnp.where(x == 0, rates[b, 0:1], rates[b, 1:2])
        rcol[b * ROWS : (b + 1) * ROWS] = jnp.broadcast_to(row, (128, ROWS)).T

    ha_copy = rcopy(tok_ref, halo, ha_s, ha_r, tok_next)

    @pl.when((s == 1) & (tok < 31))
    def _():
        ha_copy.start()

    cols = pl.ds(pl.multiple_of(c * HALF, HALF), HALF)

    @pl.when(s == 0)
    def _():
        def fill(j, carry):
            for d in range(2):
                r32 = pl.ds(pl.multiple_of(d * 256 + j * 32, 32), 32)
                r16 = pl.ds(pl.multiple_of(c * HALF + d * 128 + j * 16, 16), 16)
                wcur[d, j, 0:32] = init_ref[x, 0, r32, cols]
                wcur[d, j, 32:64] = init_ref[x, 1, r32, cols]
                wcur[d, j, 64:80] = init_ref[x, 2, r16, 0:HALF]
                wcur[d, j, 80:96] = init_ref[x, 2, r16, HALF:]
            return carry

        lax.fori_loop(0, NC, fill, 0)

    def wc_copy(d, j, src):
        dev = up if d == 0 else down
        return rcopy(src, wcur.at[d, j], wc_s.at[d, j], wc_r.at[d, j], dev)

    @pl.when(s == 1)
    def _():
        def step(i, carry):
            for d in range(2):
                hop = z - 4 if d == 0 else 7 - z
                j = i - hop

                @pl.when((j >= 0) & (j < NC))
                def _():
                    wc_copy(d, j, wcur.at[d, j]).wait_recv()

                    @pl.when(hop < 3)
                    def _():
                        wc_copy(d, j, wcur.at[d, j]).start()

            return carry

        lax.fori_loop(0, NC + 3, step, 0)

    def inner(i, carry):
        rows = pl.ds(pl.multiple_of(i * 256, 256), 256)
        kn = knb[rows]
        v = vb[rows]
        w1 = wcur[:, :, 0:32].reshape(HD, HALF)
        w3 = wcur[:, :, 32:64].reshape(HD, HALF)
        w2a = wcur[:, :, 64:80].reshape(HALF, HALF)
        w2b = wcur[:, :, 80:96].reshape(HALF, HALF)
        h1 = dot(kn, w1)
        h3 = dot(kn, w3)
        back = dot_t(v[:, :HALF], w2a) + dot_t(v[:, HALF:], w2b)
        r = rcol[rows]
        r = jnp.concatenate([r, r], 1)
        sig = jax.nn.sigmoid(h1)
        gated = h1 * sig
        back = back * r
        dbuf[rows, 0:HALF] = (back * h3 * sig * (1.0 + h1 * (1.0 - sig))).astype(bf16)
        dbuf[rows, HALF : 2 * HALF] = (back * gated).astype(bf16)
        dbuf[rows, 2 * HALF :] = (gated * h3 * r).astype(bf16)
        return carry

    lax.fori_loop(0, 8, inner, 0)

    def outer(i, carry):
        rows = pl.ds(pl.multiple_of(i * 256, 256), 256)
        g13[rows] = dot_l(knb[:, rows], dbuf[:, : 2 * HALF])
        return carry

    lax.fori_loop(0, 2, outer, 0)
    g2[...] = dot_l(dbuf[:, 2 * HALF :], vb[...])

    def own_part(d, j):
        r32 = pl.ds(pl.multiple_of(d * 256 + j * 32, 32), 32)
        r16 = pl.ds(pl.multiple_of(d * 128 + j * 16, 16), 16)
        return jnp.concatenate(
            [g13[r32, :HALF], g13[r32, HALF:], g2[r16, :HALF], g2[r16, HALF:]], 0
        )

    def rs_copy(d, j):
        dev = up if d == 0 else down
        return rcopy(sbuf.at[d, j], rbuf.at[d, j], rs_s.at[d, j], rs_r.at[d, j], dev)

    def sp_copy(d, j):
        return rcopy(ss_s.at[d, j], ss_r.at[d, j], sp_s.at[d, j], sp_r.at[d, j], mate)

    def wn_copy(d, j):
        dev = down if d == 0 else up
        w = wall.at[x, c, d, j]
        return rcopy(w, w, wn_s.at[d, j], wn_r.at[d, j], dev)

    def dp_copy(d, j):
        w = wall.at[x, c, d, j]
        return rcopy(w, w, dp_s.at[d, j], dp_r.at[d, j], mate)

    def dx_copy(d, j):
        w = wall.at[x, c, d, j]
        return rcopy(w, w, dx_s.at[d, j], dx_r.at[d, j], side)

    def df_copy(d, j):
        w = wall.at[1 - x, c, d, j]
        return rcopy(w, w, df_s.at[d, j], df_r.at[d, j], mate)

    def spread(d, j):
        dp_copy(d, j).start()
        dx_copy(d, j).start()

    def pos(d):
        return p if d == 0 else 3 - p

    def rs_stage(d, j):
        @pl.when((j >= 0) & (j < NC))
        def _():
            q = pos(d)

            @pl.when(q == 0)
            def _():
                sbuf[d, j] = own_part(d, j).astype(bf16)
                rs_copy(d, j).start()

            @pl.when((q > 0) & (q < 3))
            def _():
                rs_copy(d, j).wait_recv()
                sbuf[d, j] = (own_part(d, j) + rbuf[d, j].astype(f32)).astype(bf16)
                rs_copy(d, j).start()

            @pl.when(q == 3)
            def _():
                rs_copy(d, j).wait_recv()
                w = own_part(d, j) + rbuf[d, j].astype(f32) + wcur[d, j].astype(f32)
                wp[d, j] = w
                sq = w[0:64] * w[0:64]
                ss_s[d, j] = sq[:, :128] + sq[:, 128:]
                sp_copy(d, j).start()

    def fin_stage(d, j):
        @pl.when((j >= 0) & (j < NC) & (pos(d) == 3))
        def _():
            sp_copy(d, j).wait_recv()
            w = wp[d, j]
            r32 = pl.ds(pl.multiple_of(d * 256 + j * 32, 32), 32)
            r16 = pl.ds(pl.multiple_of(c * HALF + d * 128 + j * 16, 16), 16)
            i1 = init_ref[x, 0, r32].astype(f32)
            i3 = init_ref[x, 1, r32].astype(f32)
            i2 = init_ref[x, 2, r16].astype(f32)
            i13 = jnp.concatenate([i1, i3], 0)
            want = jnp.sqrt(jnp.mean(i13 * i13, axis=1, keepdims=True) + epsilon)
            have = jnp.sum(ss_s[d, j] + ss_r[d, j], axis=1, keepdims=True) * (1.0 / HD)
            wall[x, c, d, j, 0:64] = (w[0:64] * (want / jnp.sqrt(have + epsilon))).astype(bf16)
            want2 = jnp.sqrt(jnp.mean(i2 * i2, axis=1, keepdims=True) + epsilon)
            wa, wb = w[64:80], w[80:96]
            have2 = jnp.sum(wa * wa + wb * wb, axis=1, keepdims=True) * (1.0 / HD)
            scale2 = want2 / jnp.sqrt(have2 + epsilon)
            wall[x, c, d, j, 64:80] = (wa * scale2).astype(bf16)
            wall[x, c, d, j, 80:96] = (wb * scale2).astype(bf16)

            @pl.when(s == 0)
            def _():
                wc_copy(d, j, wall.at[x, c, d, j]).start()

            wn_copy(d, j).start()
            spread(d, j)

    def ag_stage(d, j):
        @pl.when((j >= 0) & (j < NC) & (pos(d) < 3))
        def _():
            wn_copy(d, j).wait_recv()

            @pl.when(pos(d) > 0)
            def _():
                wn_copy(d, j).start()

            spread(d, j)

    def pipe(i, carry):
        for d in range(2):
            rs_stage(d, i - pos(d))
        for d in range(2):
            fin_stage(d, i - 4)
        for d in range(2):
            ag_stage(d, i - 5 - (3 - pos(d)))
        return carry

    lax.fori_loop(0, NC + 8, pipe, 0)

    @pl.when((s == 0))
    def _():
        ha_copy.start()

    @pl.when(tok == 0)
    def _():
        halo[...] = jnp.zeros_like(halo)

    def gather(j, carry):
        for d in range(2):
            w = wall.at[1 - x, c, d, j]
            rcopy(w, w, dx_s.at[d, j], dx_r.at[d, j], side).wait_recv()
            df_copy(d, j).start()
        return carry

    lax.fori_loop(0, NC, gather, 0)

    def finish(j, carry):
        for d in range(2):
            w = wall.at[x, 1 - c, d, j]
            rcopy(w, w, dp_s.at[d, j], dp_r.at[d, j], mate).wait_recv()
            w = wall.at[1 - x, 1 - c, d, j]
            rcopy(w, w, df_s.at[d, j], df_r.at[d, j], mate).wait_recv()
            dp_copy(d, j).wait_send()
            dx_copy(d, j).wait_send()
            df_copy(d, j).wait_send()
            q = pos(d)

            @pl.when(q < 3)
            def _():
                rs_copy(d, j).wait_send()

            @pl.when(q == 3)
            def _():
                sp_copy(d, j).wait_send()

            @pl.when(q > 0)
            def _():
                wn_copy(d, j).wait_send()

            hop = z - 4 if d == 0 else 7 - z

            @pl.when(((s == 0) & (q == 3)) | ((s == 1) & (hop < 3)))
            def _():
                wc_copy(d, j, wcur.at[d, j]).wait_send()

        return carry

    lax.fori_loop(0, NC, finish, 0)
    p_send.wait_send()
    for j in range(4):
        x_send(j).wait_send()
        f_send(j).wait_send()
    for o in range(1, NH):
        lg_copy(o).wait_send()
    for i in range(3):
        rt_copy(i).wait_send()

    @pl.when(tok < 31)
    def _():
        ha_copy.wait_send()

    @pl.when(tok > 0)
    def _():
        ha_copy.wait_recv()


def apply_kernel(tok_ref, halo_ref, maps_ref, wall, out_ref, kb, vb):
    first = lax.axis_index("tok") == 0

    def one(it, carry):
        h = it
        lanes = pl.ds(pl.multiple_of(h * HD, HD), HD)

        def kv(i, cc):
            src = pl.ds(pl.multiple_of(i * 256, 256), 256)
            for ref, base in ((halo_ref, 0), (tok_ref, ROWS)):
                dst = pl.ds(pl.multiple_of(base + i * 256, 256), 256)
                xb = ref[src, lanes]
                kb[dst] = dot(xb, maps_ref[h, :, HD : 2 * HD]).astype(bf16)
                vb[dst] = dot(xb, maps_ref[h, :, 2 * HD :]).astype(bf16)
            return cc

        lax.fori_loop(0, 2, kv, 0)

        def block(i, cc):
            rows = pl.ds(pl.multiple_of(i * 256, 256), 256)
            keys = pl.ds(pl.multiple_of(i * 256, 256), 768)
            q = dot(tok_ref[rows, lanes], maps_ref[h, :, 0:HD]).astype(bf16)
            sc = dot_t(q, kb[keys]) * (HD ** (-0.5))
            ri = lax.broadcasted_iota(jnp.int32, (256, 768), 0)
            ki = lax.broadcasted_iota(jnp.int32, (256, 768), 1)
            low = jnp.where(first, WINDOW - i * 256, 0)
            mask = (ki > ri) & (ki <= ri + WINDOW) & (ki >= low)
            top = jnp.max(jnp.where(mask, sc, -1e30), axis=1, keepdims=True)
            e = jnp.where(mask, jnp.exp(sc - top), 0.0)
            probs = (e / jnp.sum(e, axis=1, keepdims=True)).astype(bf16)
            att = dot(probs, vb[keys])
            qn = rms(q)
            fast = None
            for c in range(2):
                w1 = wall[h, c, :, :, 0:32].reshape(HD, HALF)
                w3 = wall[h, c, :, :, 32:64].reshape(HD, HALF)
                w2a = wall[h, c, :, :, 64:80].reshape(HALF, HALF)
                w2b = wall[h, c, :, :, 80:96].reshape(HALF, HALF)
                a1 = dot(qn, w1)
                hq = (a1 * jax.nn.sigmoid(a1) * dot(qn, w3)).astype(bf16)
                f = jnp.concatenate([dot(hq, w2a), dot(hq, w2b)], 1)
                fast = f if fast is None else fast + f
            out_ref[rows, lanes] = (att + fast.astype(bf16).astype(f32)).astype(bf16)
            return cc

        lax.fori_loop(0, 2, block, 0)
        return carry

    lax.fori_loop(0, 2, one, 0)


def body(tokens, qkv_maps, rate_map, fast_init):
    vm = pl.BlockSpec(memory_space=pltpu.VMEM)
    dma = pltpu.SemaphoreType.DMA
    cs = dma((2, NC))
    wall, halo = pl.pallas_call(
        learn_kernel,
        out_shape=(
            jax.ShapeDtypeStruct((2, 2, 2, NC, CH, HALF), bf16),
            jax.ShapeDtypeStruct((ROWS, 2 * HD), bf16),
        ),
        in_specs=[vm] * 4,
        out_specs=(vm, vm),
        scratch_shapes=[
            pltpu.VMEM((4, ROWS, HD), bf16),
            pltpu.VMEM((4 * ROWS, HD), bf16),
            pltpu.VMEM((4 * ROWS, HD), bf16),
            pltpu.VMEM((4 * ROWS, 3 * HALF), bf16),
            pltpu.VMEM((HD, 2 * HALF), f32),
            pltpu.VMEM((HALF, HD), f32),
            pltpu.VMEM((2, NC, CH, HALF), bf16),
            pltpu.VMEM((2, NC, CH, HALF), bf16),
            pltpu.VMEM((2, NC, CH, HALF), f32),
            pltpu.VMEM((2, NC, CH, HALF), bf16),
            pltpu.VMEM((2, NC, 64, 128), f32),
            pltpu.VMEM((2, NC, 64, 128), f32),
            pltpu.VMEM((4 * ROWS, 128), f32),
            pltpu.VMEM((NH, 8, ROWS), f32),
            pltpu.VMEM((NH, 8, ROWS), f32),
            pltpu.VMEM((4, 8, ROWS), f32),
            dma, dma, dma((4,)), dma((4,)), dma((4,)), dma((4,)),
            dma((NH - 1,)), dma((NH,)), dma((3,)), dma((4,)),
            cs, cs, cs, cs, cs, cs, cs, cs,
            cs, cs, cs, cs, cs, cs, dma, dma,
        ],
        compiler_params=pltpu.CompilerParams(collective_id=0, has_side_effects=True),
        name="learn",
    )(tokens, qkv_maps, rate_map, fast_init)
    return pl.pallas_call(
        apply_kernel,
        out_shape=jax.ShapeDtypeStruct((ROWS, 2 * HD), bf16),
        in_specs=[vm] * 4,
        out_specs=vm,
        scratch_shapes=[
            pltpu.VMEM((2 * ROWS, HD), bf16),
            pltpu.VMEM((2 * ROWS, HD), bf16),
        ],
        name="apply",
    )(tokens, halo, qkv_maps, wall)


def solution(mesh):
    in_specs = (
        P("tok", "head"),
        P("head", None, None),
        P("head", None),
        P("head", None, None, None),
    )
    return jax.shard_map(
        body, mesh=mesh, in_specs=in_specs, out_specs=P("tok", "head"), check_vma=False
    )
```

time: 714 us -> 150 us (0.21)
  the two profiles are of different devices: /device:TPU:162 before, /device:TPU:227 now
where the time goes in v1:
time: 150 us
  Pallas kernels  148 us (99%)
  local copies, waits for them, and re-layouts  1.6 us (1%)
    pallas_call x1, Pallas kernels, body(): pl.pallas_call(learn_kernel, out_shape=(jax.ShapeDtypeStruct((2, 2, 2, NC...  134 us
    pallas_call x1, Pallas kernels, body(): pl.pallas_call(apply_kernel, out_shape=jax.ShapeDtypeStruct((ROWS, 2 * HD...  13.7 us

profile of v1, /device:TPU:227, one launch (start us, length us, event | category | flops | bytes accessed | tf_op | source)
XLA Modules:
  0.0 149.8 jit_solution(3306587181993962551)
XLA Ops:
  0.0 1.6 %copy.5.rmap_ref = bf16[1024,16]{1,0:T(8,128)(2,1)} copy(bf16[1024,16]{0,1:T(8,128)(2,1)} %param.6) | data formatting | bytes 65536 | tf_op args[2]
  1.6 134.4 %learn.1 = (bf16[2,2,2,8,96,256]{5,4,3,2,1,0:T(8,128)(2,1)}, bf16[512,1024]{1,0:T(8,128)(2,1)}) custom-call(bf16[512,1024]{1,0:T(8,128)(2,1)} %tok_ref.3, bf16[2,512,1536]{2,1,0:T(8,128)(2,1)} %maps_ref.3, bf16[1024,16]{1,0:T(8,128)(2,1)} %copy.5.rmap_ref, bf16[2,3,512,512]{3,2,1,0:T(8,128)(2,1)} %init_ref.1), custom_call_target="tpu_custom_call" | custom-call | tf_op jit(solution)/shard_map/learn/pallas_call | solution.py:499
  136.1 13.7 %apply.1 = bf16[512,1024]{1,0:T(8,128)(2,1)} custom-call(bf16[512,1024]{1,0:T(8,128)(2,1)} %tok_ref.3, bf16[512,1024]{1,0:T(8,128)(2,1)} %get-tuple-element.7.halo_ref, bf16[2,512,1536]{2,1,0:T(8,128)(2,1)} %maps_ref.3, bf16[2,2,2,8,96,256]{5,4,3,2,1,0:T(8,128)(2,1)} %get-tuple-element.8.wall), custom_call_target="tpu_custom_call" | custom-call | tf_op jit(solution)/shard_map/apply/pallas_call | solution.py:532

commit v2 on v0

v2 whole, which is shorter than its diff:
```python
import functools

import jax
import jax.numpy as jnp
from jax import lax
from jax.experimental import pallas as pl
from jax.experimental.pallas import tpu as pltpu
from jax.sharding import PartitionSpec as P

MESH = pl.DeviceIdType.MESH
WINDOW = 512
HD = 512
HALF = 256
ROWS = 512
NC = 8
NT = 16
SUB = 48
SKEW = 4
LAG = 2
NZ = 8
NH = 8
CH = 96

rate_base = 0.003
epsilon = 1e-06

bf16 = jnp.bfloat16
f32 = jnp.float32


def dot(a, b):
    return jnp.dot(a, b, preferred_element_type=f32)


def dot_t(a, b):
    return lax.dot_general(a, b, (((1,), (1,)), ((), ())), preferred_element_type=f32)


def dot_l(a, b):
    return lax.dot_general(a, b, (((0,), (0,)), ((), ())), preferred_element_type=f32)


def softplus(a):
    return jnp.maximum(a, 0.0) + jnp.log1p(jnp.exp(-jnp.abs(a)))


def rms(m):
    m = m.astype(f32)
    return (m * lax.rsqrt(jnp.mean(m * m, axis=-1, keepdims=True) + epsilon)).astype(bf16)


def layer_kernel(
    tok_hbm, maps_hbm, rmap_hbm, init_hbm,
    out_ref,
    tokv, maps, rmap, init, halo, wall,
    xbuf, knb, vb, dbuf, gch, rbuf, sbuf, wcur, ss_s, ss_r,
    rcol, lgs, lgr, rates, kb, vbb, att, qnb,
    in_s,
    xp_s, xp_r, xx_s, xx_r, xf_s, xf_r, lg_s, lg_r, rt_s, rt_r,
    rs_s, rs_r, sp_s, sp_r, wn_s, wn_r, wc_s, wc_r,
    dp_s, dp_r, dx_s, dx_r, df_s, df_r, ha_s, ha_r,
):
    head = lax.axis_index("head")
    tok = lax.axis_index("tok")
    z = tok // 4
    x = (tok // 2) % 2
    c = tok % 2
    p = z % 4
    s = z // 4
    b_me = x * 2 + c
    b_mate = x * 2 + 1 - c
    b_side = (1 - x) * 2 + c
    b_diag = (1 - x) * 2 + 1 - c

    def at(zz, xx, cc):
        return (head, zz * 4 + xx * 2 + cc)

    up = at((z + 1) % NZ, x, c)
    down = at((z + NZ - 1) % NZ, x, c)
    mate = at(z, x, 1 - c)
    side = at(z, 1 - x, c)
    diag = at(z, 1 - x, 1 - c)
    tok_next = (head, (tok + 1) % 32)
    tok_prev = (head, (tok + 31) % 32)

    loads = [
        pltpu.make_async_copy(tok_hbm, tokv, in_s.at[0]),
        pltpu.make_async_copy(rmap_hbm, rmap, in_s.at[1]),
        pltpu.make_async_copy(maps_hbm.at[x], maps.at[x], in_s.at[2]),
        pltpu.make_async_copy(init_hbm.at[x], init, in_s.at[3]),
        pltpu.make_async_copy(maps_hbm.at[1 - x], maps.at[1 - x], in_s.at[4]),
    ]
    for load in loads:
        load.start()

    barrier = pltpu.get_barrier_semaphore()
    peers = [up, down, mate, side, diag, tok_next, tok_prev]
    peers += [((head + o) % NH, tok) for o in range(1, NH)]
    for peer in peers:
        pl.semaphore_signal(barrier, inc=1, device_id=peer, device_id_type=MESH)
    pl.semaphore_wait(barrier, len(peers))

    def rcopy(src, dst, ssem, rsem, dev):
        return pltpu.make_async_remote_copy(
            src_ref=src, dst_ref=dst, send_sem=ssem, recv_sem=rsem,
            device_id=dev, device_id_type=MESH,
        )

    mine = pl.ds(pl.multiple_of(x * HD, HD), HD)
    other = pl.ds(pl.multiple_of((1 - x) * HD, HD), HD)

    def r128(j):
        return pl.ds(pl.multiple_of(j * 128, 128), 128)

    def x_copy(j, b):
        return rcopy(
            tok_hbm.at[r128(j), other], xbuf.at[b, r128(j)], xx_s.at[j], xx_r.at[j], side
        )

    def f_copy(j, b):
        blk = xbuf.at[b, r128(j)]
        return rcopy(blk, blk, xf_s.at[j], xf_r.at[j], mate)

    def p_copy(b):
        return rcopy(tok_hbm.at[:, mine], xbuf.at[b], xp_s, xp_r, mate)

    for j in range(4):
        x_copy(j, b_me).start()
    p_copy(b_me).start()

    loads[0].wait()
    loads[1].wait()
    part = dot_t(rmap[...], tokv[...])
    for q in range(NH):
        lgs[q] = jnp.concatenate([part[2 * q : 2 * q + 2], jnp.zeros((6, ROWS), f32)], 0)

    def lg_copy(o):
        peer = (head + o) % NH
        return rcopy(lgs.at[peer], lgr.at[head], lg_s.at[o - 1], lg_r.at[head], (peer, tok))

    def lg_wait(o):
        src = (head + o) % NH
        return rcopy(lgs.at[src], lgr.at[src], lg_s.at[o - 1], lg_r.at[src], (src, tok))

    for o in range(1, NH):
        lg_copy(o).start()
    lgr[head] = lgs[head]
    xbuf[b_me] = tokv[:, mine]

    cols = pl.ds(pl.multiple_of(c * HALF, HALF), HALF)
    loads[3].wait()

    @pl.when(s == 0)
    def _():
        def fill(j, carry):
            for d in range(2):
                r32 = pl.ds(pl.multiple_of(d * 256 + j * 32, 32), 32)
                r16 = pl.ds(pl.multiple_of(c * HALF + d * 128 + j * 16, 16), 16)
                wcur[d, j, 0:32] = init[0, r32, cols]
                wcur[d, j, 32:64] = init[1, r32, cols]
                wcur[d, j, 64:80] = init[2, r16, 0:HALF]
                wcur[d, j, 80:96] = init[2, r16, HALF:]
            return carry

        lax.fori_loop(0, NC, fill, 0)

    loads[2].wait()

    def keys_values(b, r, n):
        rows = pl.ds(pl.multiple_of(r, n), n)
        xb = xbuf[b, rows]
        out = pl.ds(pl.multiple_of(b * ROWS + r, n), n)
        knb[out] = rms(dot(xb, maps[x, :, HD : 2 * HD]).astype(bf16))
        vb[out] = dot(xb, maps[x, :, 2 * HD :]).astype(bf16)

    def inner(row, n):
        rows = pl.ds(pl.multiple_of(row, n), n)
        kn = knb[rows]
        v = vb[rows]
        w1 = wcur[:, :, 0:32].reshape(HD, HALF)
        w3 = wcur[:, :, 32:64].reshape(HD, HALF)
        w2a = wcur[:, :, 64:80].reshape(HALF, HALF)
        w2b = wcur[:, :, 80:96].reshape(HALF, HALF)
        h1 = dot(kn, w1)
        h3 = dot(kn, w3)
        back = dot_t(v[:, :HALF], w2a) + dot_t(v[:, HALF:], w2b)
        r = rcol[rows]
        r = jnp.concatenate([r, r], 1)
        sig = jax.nn.sigmoid(h1)
        gated = h1 * sig
        back = back * r
        dbuf[rows, 0:HALF] = (back * h3 * sig * (1.0 + h1 * (1.0 - sig))).astype(bf16)
        dbuf[rows, HALF : 2 * HALF] = (back * gated).astype(bf16)
        dbuf[rows, 2 * HALF :] = (gated * h3 * r).astype(bf16)

    def outer(d, row, n, add):
        rows = pl.ds(pl.multiple_of(row, n), n)
        k_cols = pl.ds(pl.multiple_of(d * 256, 256), 256)
        h_cols = pl.ds(pl.multiple_of(2 * HALF + d * 128, 128), 128)
        a = dot_l(knb[rows, k_cols], dbuf[rows, 0 : 2 * HALF])
        e = dot_l(dbuf[rows, h_cols], vb[rows])
        parts = [
            (0, 32, a[:, :HALF]), (32, 32, a[:, HALF:]), (64, 16, e[:, :HALF]), (80, 16, e[:, HALF:])
        ]
        for lo, m, g in parts:
            g = g.reshape(NC, m, HALF)
            if add:
                g = g + gch[d, :, lo : lo + m]
            gch[d, :, lo : lo + m] = g

    def fill_rate(b):
        row = jnp.where(x == 0, rates[b, 0:1], rates[b, 1:2])
        rcol[pl.ds(pl.multiple_of(b * ROWS, ROWS), ROWS)] = jnp.broadcast_to(row, (128, ROWS)).T

    def kv_block(b):
        def step(i, carry):
            keys_values(b, i * 256, 256)
            return carry

        lax.fori_loop(0, 2, step, 0)

    def inner_block(row, n):
        def step(i, carry):
            inner(row + i * 256, 256)
            return carry

        lax.fori_loop(0, n // 256, step, 0)

    kv_block(b_me)
    for o in range(1, NH):
        lg_wait(o).wait_recv()
    total = lgr[0]
    for q in range(1, NH):
        total = total + lgr[q]
    rates[b_me] = (rate_base * softplus(total)).astype(bf16).astype(f32)
    group = [(mate, b_mate), (side, b_side), (diag, b_diag)]

    def rt_copy(i):
        dev, _ = group[i]
        return rcopy(rates.at[b_me], rates.at[b_me], rt_s.at[i], rt_r.at[b_me], dev)

    def rt_wait(i):
        dev, src = group[i]
        return rcopy(rates.at[src], rates.at[src], rt_s.at[i], rt_r.at[src], dev)

    for i in range(3):
        rt_copy(i).start()
    fill_rate(b_me)
    p_copy(b_mate).wait_recv()
    kv_block(b_mate)
    for i in range(3):
        rt_wait(i).wait_recv()
        fill_rate(group[i][1])

    @pl.when(s == 0)
    def _():
        inner_block(x * 2 * ROWS, 2 * ROWS)
        for d in range(2):
            outer(d, x * 2 * ROWS, 2 * ROWS, False)

    def arrive(j, carry):
        @pl.when(j < 4)
        def _():
            x_copy(j, b_side).wait_recv()
            f_copy(j, b_side).start()
            keys_values(b_side, j * 128, 128)

            @pl.when(s == 0)
            def _():
                inner(b_side * ROWS + j * 128, 128)

        @pl.when(j > 0)
        def _():
            f_copy(j - 1, b_diag).wait_recv()
            keys_values(b_diag, (j - 1) * 128, 128)

            @pl.when(s == 0)
            def _():
                inner(b_diag * ROWS + (j - 1) * 128, 128)

        return carry

    lax.fori_loop(0, 5, arrive, 0)

    ha_copy = rcopy(tokv, halo, ha_s, ha_r, tok_next)
    late = (z < 3) & (b_me == 3)

    @pl.when((tok < 31) & jnp.logical_not(late))
    def _():
        ha_copy.start()

    def attention():
        @pl.when(tok == 0)
        def _():
            halo[...] = jnp.zeros_like(halo)

        @pl.when(tok > 0)
        def _():
            ha_copy.wait_recv()

        def one(h, carry):
            lanes = pl.ds(pl.multiple_of(h * HD, HD), HD)

            def kv(i, cc):
                src = pl.ds(pl.multiple_of(i * 256, 256), 256)
                for ref, base in ((halo, 0), (tokv, ROWS)):
                    dst = pl.ds(pl.multiple_of(base + i * 256, 256), 256)
                    xb = ref[src, lanes]
                    kb[dst] = dot(xb, maps[h, :, HD : 2 * HD]).astype(bf16)
                    vbb[dst] = dot(xb, maps[h, :, 2 * HD :]).astype(bf16)
                return cc

            lax.fori_loop(0, 2, kv, 0)

            def block(i, cc):
                rows = pl.ds(pl.multiple_of(i * 256, 256), 256)
                keys = pl.ds(pl.multiple_of(i * 256, 256), 768)
                q = dot(tokv[rows, lanes], maps[h, :, 0:HD]).astype(bf16)
                qnb[rows, lanes] = rms(q)
                sc = dot_t(q, kb[keys]) * (HD ** (-0.5))
                ri = lax.broadcasted_iota(jnp.int32, (256, 768), 0)
                ki = lax.broadcasted_iota(jnp.int32, (256, 768), 1)
                low = jnp.where(tok == 0, WINDOW - i * 256, 0)
                mask = (ki > ri) & (ki <= ri + WINDOW) & (ki >= low)
                top = jnp.max(jnp.where(mask, sc, -1e30), axis=1, keepdims=True)
                e = jnp.where(mask, jnp.exp(sc - top), 0.0)
                probs = (e / jnp.sum(e, axis=1, keepdims=True)).astype(bf16)
                att[rows, lanes] = dot(probs, vbb[keys])
                return cc

            lax.fori_loop(0, 2, block, 0)
            return carry

        lax.fori_loop(0, 2, one, 0)

    def sub(t):
        return t // 2, pl.ds(pl.multiple_of((t % 2) * SUB, 16), SUB)

    def wc_copy(d, t, src):
        j, r = sub(t)
        dev = up if d == 0 else down
        return rcopy(src.at[d, j, r], wcur.at[d, j, r], wc_s.at[d, t], wc_r.at[d, t], dev)

    @pl.when(s == 1)
    def _():
        loads[4].wait()
        attention()

        def step(i, carry):
            for d in range(2):
                hop = z - 4 if d == 0 else 7 - z
                t = i - SKEW * hop

                @pl.when((t >= 0) & (t < NT))
                def _():
                    wc_copy(d, t, wcur).wait_recv()

                    @pl.when(hop < 3)
                    def _():
                        wc_copy(d, t, wcur).start()

            return carry

        lax.fori_loop(0, NT + 3 * SKEW, step, 0)
        inner_block(0, 4 * ROWS)

    def rs_copy(d, t):
        j, r = sub(t)
        dev = up if d == 0 else down
        return rcopy(sbuf.at[d, j, r], rbuf.at[d, j, r], rs_s.at[d, t], rs_r.at[d, t], dev)

    def pos(d):
        return p if d == 0 else 3 - p

    def send_first(d):
        @pl.when(pos(d) == 0)
        def _():
            def step(t, carry):
                j, r = sub(t)
                sbuf[d, j, r] = gch[d, j, r].astype(bf16)
                rs_copy(d, t).start()
                return carry

            lax.fori_loop(0, NT, step, 0)

    def grads(d):
        @pl.when(s == 0)
        def _():
            outer(d, (1 - x) * 2 * ROWS, 2 * ROWS, True)

        @pl.when(s == 1)
        def _():
            outer(d, 0, 4 * ROWS, False)

        send_first(d)

    @pl.when(p < 2)
    def _():
        grads(0)
        grads(1)

    @pl.when(p >= 2)
    def _():
        grads(1)
        grads(0)

    def sp_copy(d, t):
        return rcopy(ss_s.at[d, t], ss_r.at[d, t], sp_s.at[d, t], sp_r.at[d, t], mate)

    def wn_copy(d, t):
        j, r = sub(t)
        dev = down if d == 0 else up
        w = wall.at[x, c, d, j, r]
        return rcopy(w, w, wn_s.at[d, t], wn_r.at[d, t], dev)

    def spread_copy(d, t, xx, cc, ssem, rsem, dev):
        j, r = sub(t)
        w = wall.at[xx, cc, d, j, r]
        return rcopy(w, w, ssem.at[d, t], rsem.at[d, t], dev)

    def dp_copy(d, t, cc):
        return spread_copy(d, t, x, cc, dp_s, dp_r, mate)

    def dx_copy(d, t, xx):
        return spread_copy(d, t, xx, c, dx_s, dx_r, side)

    def df_copy(d, t, cc):
        return spread_copy(d, t, 1 - x, cc, df_s, df_r, mate)

    def spread(d, t):
        dx_copy(d, t, x).start()
        dp_copy(d, t, c).start()

    def rs_stage(d, t):
        q = pos(d)

        @pl.when((t >= 0) & (t < NT) & (q > 0))
        def _():
            j, r = sub(t)
            rs_copy(d, t).wait_recv()
            tot = gch[d, j, r] + rbuf[d, j, r].astype(f32)

            @pl.when(q < 3)
            def _():
                sbuf[d, j, r] = tot.astype(bf16)
                rs_copy(d, t).start()

            @pl.when(q == 3)
            def _():
                w = tot + wcur[d, j, r].astype(f32)
                gch[d, j, r] = w
                sq = w * w
                ss_s[d, t] = sq[:, :128] + sq[:, 128:]
                sp_copy(d, t).start()

    def scale_of(init_rows, have):
        m = init_rows.astype(f32)
        want = jnp.sqrt(jnp.mean(m * m, axis=1, keepdims=True) + epsilon)
        return want / jnp.sqrt(have * (1.0 / HD) + epsilon)

    def fin_stage(d, t):
        @pl.when((t >= 0) & (t < NT) & (pos(d) == 3))
        def _():
            sp_copy(d, t).wait_recv()
            j = t // 2
            have = jnp.sum(ss_s[d, t] + ss_r[d, t], axis=1, keepdims=True)
            r32 = pl.ds(pl.multiple_of(d * 256 + j * 32, 32), 32)
            r16a = pl.ds(pl.multiple_of(d * 256 + j * 32, 16), 16)
            r16b = pl.ds(pl.multiple_of(d * 256 + j * 32 + 16, 16), 16)
            r16 = pl.ds(pl.multiple_of(c * HALF + d * 128 + j * 16, 16), 16)

            @pl.when(t % 2 == 0)
            def _():
                w = gch[d, j, 0:48]
                rows = jnp.concatenate([init[0, r32], init[1, r16a]], 0)
                wall[x, c, d, j, 0:48] = (w * scale_of(rows, have)).astype(bf16)

            @pl.when(t % 2 == 1)
            def _():
                w = gch[d, j, 48:64]
                wall[x, c, d, j, 48:64] = (w * scale_of(init[1, r16b], have[0:16])).astype(bf16)
                wa = gch[d, j, 64:80]
                wb = gch[d, j, 80:96]
                sc = scale_of(init[2, r16], jnp.sum(wa * wa + wb * wb, axis=1, keepdims=True))
                wall[x, c, d, j, 64:80] = (wa * sc).astype(bf16)
                wall[x, c, d, j, 80:96] = (wb * sc).astype(bf16)

            @pl.when(s == 0)
            def _():
                wc_copy(d, t, wall.at[x, c]).start()

            wn_copy(d, t).start()
            spread(d, t)

    def ag_stage(d, t):
        @pl.when((t >= 0) & (t < NT) & (pos(d) < 3))
        def _():
            wn_copy(d, t).wait_recv()

            @pl.when(pos(d) > 0)
            def _():
                wn_copy(d, t).start()

            spread(d, t)

    def pipe(i, carry):
        for d in range(2):
            rs_stage(d, i - SKEW * (pos(d) - 1))
        for d in range(2):
            fin_stage(d, i - 2 * SKEW - LAG)
        for d in range(2):
            ag_stage(d, i - 2 * SKEW - LAG - SKEW * (3 - pos(d)))
        return carry

    lax.fori_loop(0, NT + 5 * SKEW + LAG, pipe, 0)

    @pl.when(late)
    def _():
        ha_copy.start()

    def hand_on(t, carry):
        for d in range(2):
            dx_copy(d, t, 1 - x).wait_recv()
            df_copy(d, t, c).start()
        return carry

    lax.fori_loop(0, NT, hand_on, 0)

    @pl.when(s == 0)
    def _():
        loads[4].wait()
        attention()

    def apply_head(h):
        lanes = pl.ds(pl.multiple_of(h * HD, HD), HD)

        def block(i, cc):
            rows = pl.ds(pl.multiple_of(i * 256, 256), 256)
            qn = qnb[rows, lanes]
            fast = None
            for e in range(2):
                w1 = wall[h, e, :, :, 0:32].reshape(HD, HALF)
                w3 = wall[h, e, :, :, 32:64].reshape(HD, HALF)
                w2a = wall[h, e, :, :, 64:80].reshape(HALF, HALF)
                w2b = wall[h, e, :, :, 80:96].reshape(HALF, HALF)
                a1 = dot(qn, w1)
                hq = (a1 * jax.nn.sigmoid(a1) * dot(qn, w3)).astype(bf16)
                f = jnp.concatenate([dot(hq, w2a), dot(hq, w2b)], 1)
                fast = f if fast is None else fast + f
            out_ref[rows, lanes] = (att[rows, lanes] + fast.astype(bf16).astype(f32)).astype(bf16)
            return cc

        lax.fori_loop(0, 2, block, 0)

    def own_head(t, carry):
        for d in range(2):
            dp_copy(d, t, 1 - c).wait_recv()
        return carry

    lax.fori_loop(0, NT, own_head, 0)
    apply_head(x)

    def other_head(t, carry):
        for d in range(2):
            df_copy(d, t, 1 - c).wait_recv()
        return carry

    lax.fori_loop(0, NT, other_head, 0)
    apply_head(1 - x)

    def finish(t, carry):
        for d in range(2):
            dp_copy(d, t, c).wait_send()
            dx_copy(d, t, x).wait_send()
            df_copy(d, t, c).wait_send()
            q = pos(d)

            @pl.when(q < 3)
            def _():
                rs_copy(d, t).wait_send()

            @pl.when(q == 3)
            def _():
                sp_copy(d, t).wait_send()

            @pl.when(q > 0)
            def _():
                wn_copy(d, t).wait_send()

            hop = z - 4 if d == 0 else 7 - z

            @pl.when(((s == 0) & (q == 3)) | ((s == 1) & (hop < 3)))
            def _():
                wc_copy(d, t, wcur).wait_send()

        return carry

    lax.fori_loop(0, NT, finish, 0)
    p_copy(b_me).wait_send()
    for j in range(4):
        x_copy(j, b_me).wait_send()
        f_copy(j, b_side).wait_send()
    for o in range(1, NH):
        lg_copy(o).wait_send()
    for i in range(3):
        rt_copy(i).wait_send()

    @pl.when(tok < 31)
    def _():
        ha_copy.wait_send()


def body(tokens, qkv_maps, rate_map, fast_init):
    vm = pl.BlockSpec(memory_space=pltpu.VMEM)
    hbm = pl.BlockSpec(memory_space=pl.ANY)
    dma = pltpu.SemaphoreType.DMA
    cs = dma((2, NT))
    V = pltpu.VMEM
    chunk = (2, NC, CH, HALF)
    return pl.pallas_call(
        layer_kernel,
        out_shape=jax.ShapeDtypeStruct((ROWS, 2 * HD), bf16),
        in_specs=[hbm] * 4,
        out_specs=vm,
        scratch_shapes=[
            V((ROWS, 2 * HD), bf16),
            V((2, HD, 3 * HD), bf16),
            V((2 * NH, 2 * HD), bf16),
            V((3, HD, HD), bf16),
            V((ROWS, 2 * HD), bf16),
            V((2, 2) + chunk, bf16),
            V((4, ROWS, HD), bf16),
            V((4 * ROWS, HD), bf16),
            V((4 * ROWS, HD), bf16),
            V((4 * ROWS, 3 * HALF), bf16),
            V(chunk, f32),
            V(chunk, bf16),
            V(chunk, bf16),
            V(chunk, bf16),
            V((2, NT, SUB, 128), f32),
            V((2, NT, SUB, 128), f32),
            V((4 * ROWS, 128), f32),
            V((NH, 8, ROWS), f32),
            V((NH, 8, ROWS), f32),
            V((4, 8, ROWS), f32),
            V((2 * ROWS, HD), bf16),
            V((2 * ROWS, HD), bf16),
            V((ROWS, 2 * HD), f32),
            V((ROWS, 2 * HD), bf16),
            dma((5,)),
            dma, dma, dma((4,)), dma((4,)), dma((4,)), dma((4,)),
            dma((NH - 1,)), dma((NH,)), dma((3,)), dma((4,)),
            cs, cs, cs, cs, cs, cs, cs, cs,
            cs, cs, cs, cs, cs, cs, dma, dma,
        ],
        compiler_params=pltpu.CompilerParams(collective_id=0, has_side_effects=True),
        name="layer",
    )(tokens, qkv_maps, rate_map.T, fast_init)


def solution(mesh):
    in_specs = (
        P("tok", "head"),
        P("head", None, None),
        P("head", None),
        P("head", None, None, None),
    )
    return jax.shard_map(
        body, mesh=mesh, in_specs=in_specs, out_specs=P("tok", "head"), check_vma=False
    )
```

time: 714 us -> 118 us (0.17); the launches traced: 707 us -> 118 us
  waiting for transfers between devices: 504 us -> 0 us
  Pallas kernels: 0 us -> 116 us
  starting transfers between devices: 57.9 us -> 0 us
  blocking collectives: 41.1 us -> 0 us
  local copies, waits for them, and re-layouts: 36.9 us -> 2.26 us
  matrix products: 29.6 us -> 0 us
  other arithmetic: 22.9 us -> 0 us
  between operations: 14.5 us -> 0.01 us
    psum x2 -> x0, waiting for transfers between devices: 429 us -> none  [update_weights(): lax.psum(partial_value.astype(jnp.bfloat16), 'tok').astype(jnp.float32)]
    pallas_call x0 -> x1, Pallas kernels: none -> 116 us  [body(): pl.pallas_call(layer_kernel, out_shape=jax.ShapeDtypeStruct((ROWS, 2 * HD...]
    all_to_all x5 -> x0, waiting for transfers between devices: 75.1 us -> none  [the longest x1 21.7 us: body(): lax.all_to_all(q_norm, 'tok', split_axis=0, concat_axis=0, tiled=True)]
    all_to_all x5 -> x0, starting transfers between devices: 55.6 us -> none  [the longest x1 15.7 us: body(): lax.all_to_all(jnp.concatenate(outputs, 0), 'tok', split_axis=0, concat_a...]
    unnamed x1 -> x0, blocking collectives: 41.1 us -> none
    dot_general x20 -> x0, matrix products: 29.6 us -> none  [the longest x1 5.6 us: band_attention(): jnp.einsum('hqk,khd->qhd', probs, value_rows, preferred_element_type=jnp....]
    slice x5 -> x0, local copies, waits for them, and re-layouts: 12.2 us -> none  [the longest x1 3.85 us: body(): value_rows = projected[:, :, 2 * head_width:].astype(jnp.bfloat16)]
    convert_element_type x4 -> x0, local copies, waits for them, and re-layouts: 7.64 us -> none  [the longest x1 3.81 us: body(): k_norm = rms_rows(key_rows).astype(jnp.bfloat16)]
  transfers between devices with their start and end apart: 8 -> 0, of which waited for: 6 -> 0; matrix products, arithmetic and copies ran while one was open for 8% -> 0% of each run, Pallas kernels for 0% -> 0%
where the time goes in v2:
time: 118 us
  Pallas kernels  116 us (98%)
  local copies, waits for them, and re-layouts  2.26 us (2%)
    pallas_call x1, Pallas kernels, body(): pl.pallas_call(layer_kernel, out_shape=jax.ShapeDtypeStruct((ROWS, 2 * HD...  116 us

profile of v2, /device:TPU:162, one launch (start us, length us, event | category | flops | bytes accessed | tf_op | source)
XLA Modules:
  0.0 117.9 jit_solution(1711698808558922492)
XLA Ops:
  0.0 115.6 %layer.1 = bf16[512,1024]{1,0:T(8,128)(2,1)} custom-call(bf16[512,1024]{1,0:T(8,128)(2,1)} %tok_hbm.1, bf16[2,512,1536]{2,1,0:T(8,128)(2,1)} %maps_hbm.1, bf16[16,1024]{1,0:T(8,128)(2,1)} %bitcast.1, bf16[2,3,512,512]{3,2,1,0:T(8,128)(2,1)} %init_hbm.1), custom_call_target="tpu_custom_call" | custom-call | tf_op jit(solution)/shard_map/layer/pallas_call | solution.py:620
  115.6 2.3 %copy.6 = bf16[512,1024]{1,0:T(8,128)(2,1)} copy(bf16[512,1024]{1,0:T(8,128)(2,1)} %layer.1) | data formatting | bytes 2097152
